TPU v7x, 256 devices: a whole 4x4x8 slice. The times are simulated.
256 devices in a mesh: sect: 64 (over z, y, core), tp: 4 (over x).
Axes of the slice: x: 4, y: 4, z: 8, core: 2. Of those that a mesh axis runs over, the one named last changes fastest.
Arguments:
- item_hidden: bfloat16 [4096, 4096], P('sect', 'tp'), may hold values from -40 to 40
- item_gain: bfloat16 [4096], P('tp'), may hold values from 0.25 to 1.75
- send_item: int32 [64, 64, 4], P('sect'), may hold values from -1 to 63, as said below
- pos_slot: int32 [256, 192], P('sect'), may hold values from 0 to 255, as said below
- hist_len: int32 [256], P('sect'), may hold values from 64 to 128, as said below
- user_gain: bfloat16 [4096], P('tp'), may hold values from 0.25 to 1.75
- query_weight: bfloat16 [4096, 4096], P('tp', 'sect'), may hold values from -0.09375 to 0.09375
Outputs:
- item_grad: float32 [4096, 4096], P('sect', 'tp')
- user_loss: float32 [256], P('sect')
Inputs may be any that keep to these rules, and one draw needn't show every extreme that they name: `send_item`: entry [o, r, s] names item o * 64 + value, owned by device o and sent to reader r, or is -1 for an empty slot. Within one (o, r) block the named items are distinct and the filled slots come first; at least half of the 4 slots (rounded down, and at least one) are filled. In every draw some reader gets 4 filled slots from every owner. `pos_slot`: entry [u, j] names a filled slot of the buffer of the device holding user u, in the order o * 4 + s; every filled slot is named by some candidate or some history position below that user's length. `hist_len`: every device's block of 4 users holds a user of length 128.
All inputs are finite; a program needn't handle non-finite values.
Results may differ from a plain program's by a relative error of at most 0.015.
Values may be sent and summed in bfloat16 or wider, within the bound.
A program may use at most 128 MiB of HBM per device.

v0:
```python
import jax
import jax.numpy as jnp
from jax import lax
from jax.sharding import PartitionSpec as P

D = 4096
HD = 128
CAND = 64
NORM_FLOOR = 1e-06
LOGIT_SOFTNESS = 20.0


def head_norm(values, head_count):
    shaped = values.reshape(values.shape[:-1] + (head_count, values.shape[-1] // head_count))
    return shaped * lax.rsqrt(jnp.mean(shaped * shaped, axis=-1, keepdims=True) + NORM_FLOOR)


def causal_mask(lengths, history_span):
    position = jnp.arange(history_span)
    allowed = (position[None, :] <= position[:, None])[None] & (
        position[None, None, :] < lengths[:, None, None]
    )
    return allowed.astype(jnp.float32)


def attend(query_rows, normed_rows, attend_mask):
    head_count = query_rows.shape[-1] // HD
    query_heads = head_norm(query_rows, head_count).astype(jnp.bfloat16)
    key_heads = head_norm(normed_rows, head_count).astype(jnp.bfloat16)
    value_heads = normed_rows.astype(jnp.bfloat16).reshape(query_heads.shape)
    scores = jnp.einsum(
        "uihd,ujhd->uhij", query_heads, key_heads, preferred_element_type=jnp.float32
    ) * HD ** (-0.5)
    weights = jnp.exp(scores) * attend_mask[:, None]
    weights = weights / jnp.sum(weights, axis=-1, keepdims=True)
    mixed_rows = jnp.einsum(
        "uhij,ujhd->uihd",
        weights.astype(jnp.bfloat16),
        value_heads,
        preferred_element_type=jnp.float32,
    )
    return mixed_rows.reshape(query_rows.shape)


def score_parts(mixed_rows, history_rows, cand_rows):
    outputs = history_rows + mixed_rows
    follow = jnp.concatenate([history_rows[:, 1:], jnp.zeros_like(history_rows[:, :1])], axis=1)
    own_squares = jnp.sum(outputs * outputs, axis=-1)
    positive_dot_products = jnp.sum(outputs * follow, axis=-1)
    negative_dot_products = jnp.einsum(
        "uif,ucf->uic", outputs, cand_rows, precision=lax.Precision.HIGHEST
    )
    return (own_squares, positive_dot_products, negative_dot_products)


def user_losses(
    own_squares,
    positive_dot_products,
    negative_dot_products,
    next_item_square_sums,
    candidate_square_sums,
    lengths,
):
    reciprocal_norm = lax.rsqrt(own_squares + NORM_FLOOR)
    positive_target_logit = (
        LOGIT_SOFTNESS
        * positive_dot_products
        * reciprocal_norm
        * lax.rsqrt(next_item_square_sums + NORM_FLOOR)
    )
    negative_score_logits = (
        LOGIT_SOFTNESS
        * negative_dot_products
        * reciprocal_norm[..., None]
        * lax.rsqrt(candidate_square_sums + NORM_FLOOR)[:, None, :]
    )
    partition = jnp.exp(positive_target_logit) + jnp.sum(jnp.exp(negative_score_logits), axis=-1)
    terms = jnp.log(partition) - positive_target_logit
    position = jnp.arange(own_squares.shape[1])
    allowed = position[None, :] < lengths[:, None] - 1
    return jnp.sum(jnp.where(allowed, terms, 0.0), axis=-1) / (lengths - 1).astype(jnp.float32)


def slot_norm(slot_rows, slot_squares, gain_row):
    return slot_rows * lax.rsqrt(slot_squares / D + NORM_FLOOR)[:, None] * gain_row


def segment_rows(values, places, count):
    return jax.ops.segment_sum(
        values.reshape((-1,) + values.shape[2:]), places.reshape(-1), num_segments=count
    )


def local(item_hidden, item_gain, send_item, pos_slot, hist_len, user_gain, query_weight):
    hidden = item_hidden.astype(jnp.float32)
    item_squares = lax.psum(jnp.sum(hidden * hidden, axis=1), "tp")
    embedded = (
        hidden * lax.rsqrt(item_squares / D + NORM_FLOOR)[:, None] * item_gain.astype(jnp.float32)
    ).astype(jnp.bfloat16)
    send_slots = send_item[0]
    vacant = send_slots < 0
    picked = jnp.take(embedded, jnp.where(vacant, 0, send_slots), axis=0)
    outgoing = jnp.where(vacant[..., None], jnp.zeros((), jnp.bfloat16), picked)
    arrived = lax.all_to_all(outgoing, "sect", split_axis=0, concat_axis=0, tiled=True)
    feature_count = arrived.shape[-1]
    slot_rows = arrived.reshape(-1, feature_count).astype(jnp.float32)
    slot_count = slot_rows.shape[0]
    slot_squares = lax.psum(jnp.sum(slot_rows * slot_rows, axis=1), "tp")
    gain_row = user_gain.astype(jnp.float32)

    def norm_only(rows_in, squares_in):
        return slot_norm(rows_in, squares_in, gain_row)

    normed_slots, norm_back = jax.vjp(norm_only, slot_rows, slot_squares)
    normed_low = normed_slots.astype(jnp.bfloat16)
    partial_query = jnp.dot(
        normed_low,
        lax.all_gather(query_weight, "sect", axis=1, tiled=True),
        preferred_element_type=jnp.float32,
    )
    query_slots = lax.psum_scatter(
        partial_query.astype(jnp.bfloat16), "tp", scatter_dimension=1, tiled=True
    ).astype(jnp.float32)
    history_span = pos_slot.shape[1] - CAND
    hist_places = pos_slot[:, :history_span]
    cand_places = pos_slot[:, history_span:]
    follow_places = jnp.concatenate([hist_places[:, 1:], hist_places[:, :1]], axis=1)
    history_rows = slot_rows[hist_places]
    cand_rows = slot_rows[cand_places]
    normed_rows = normed_low[hist_places].astype(jnp.float32)
    query_rows = query_slots[hist_places]
    attend_mask = causal_mask(hist_len, history_span)

    def attend_only(query_in, normed_in):
        return attend(query_in, normed_in, attend_mask)

    mixed_rows, attend_back = jax.vjp(attend_only, query_rows, normed_rows)
    partial_stats, parts_back = jax.vjp(score_parts, mixed_rows, history_rows, cand_rows)
    own_squares, positive_dot_products, negative_dot_products = (
        lax.psum(partial_stats[0].astype(jnp.bfloat16), "tp").astype(jnp.float32),
        lax.psum(partial_stats[1].astype(jnp.bfloat16), "tp").astype(jnp.float32),
        lax.psum(partial_stats[2].astype(jnp.bfloat16), "tp").astype(jnp.float32),
    )
    next_item_square_sums = slot_squares[follow_places]
    candidate_square_sums = slot_squares[cand_places]

    def loss_only(own_in, hit_in, neg_in, follow_in, cand_in):
        return user_losses(own_in, hit_in, neg_in, follow_in, cand_in, hist_len)

    losses, loss_back = jax.vjp(
        loss_only,
        own_squares,
        positive_dot_products,
        negative_dot_products,
        next_item_square_sums,
        candidate_square_sums,
    )
    grad_own, grad_hit, grad_neg, grad_follow, grad_cand = loss_back(
        jnp.full(losses.shape, float(D), jnp.float32)
    )
    grad_mixed, grad_history, grad_cands = parts_back((grad_own, grad_hit, grad_neg))
    grad_query, grad_normed = attend_back(grad_mixed)
    grad_slots = segment_rows(grad_history, hist_places, slot_count) + segment_rows(
        grad_cands, cand_places, slot_count
    )
    grad_squares = segment_rows(grad_follow, follow_places, slot_count) + segment_rows(
        grad_cand, cand_places, slot_count
    )
    grad_norm_slots = segment_rows(grad_normed, hist_places, slot_count)
    grad_query_slots = segment_rows(grad_query, hist_places, slot_count)
    every_query = lax.all_gather(grad_query_slots.astype(jnp.bfloat16), "tp", axis=1, tiled=True)
    grad_from_query = lax.dot_general(
        every_query,
        lax.all_gather(query_weight, "sect", axis=1, tiled=True),
        (((1,), (1,)), ((), ())),
        preferred_element_type=jnp.float32,
    )
    grad_norm_slots = grad_norm_slots + grad_from_query
    back_rows, back_squares = norm_back(grad_norm_slots)
    back_squares = lax.psum(back_squares, "tp")
    grad_slots = grad_slots + back_rows + 2.0 * slot_rows * (grad_squares + back_squares)[:, None]
    returned = lax.all_to_all(
        grad_slots.reshape(arrived.shape).astype(jnp.bfloat16),
        "sect",
        split_axis=0,
        concat_axis=0,
        tiled=True,
    ).astype(jnp.float32)
    item_count = embedded.shape[0]
    targets = jnp.where(vacant, item_count, send_slots).reshape(-1)
    item_grad = jax.ops.segment_sum(
        returned.reshape(-1, feature_count), targets, num_segments=item_count + 1
    )[:item_count]
    return (item_grad, losses)


def solution(mesh):
    placed = (
        P("sect", "tp"),
        P("tp"),
        P("sect", None, None),
        P("sect", None),
        P("sect"),
        P("tp"),
        P("tp", "sect"),
    )
    return jax.shard_map(
        local, mesh=mesh, in_specs=placed, out_specs=(P("sect", "tp"), P("sect")), check_vma=False
    )
```

profile of v0, /device:TPU:1, one launch (start us, length us, event | category | flops | bytes accessed | tf_op | source)
XLA Modules:
  0.0 333.5 jit_solution(12200618832667628850)
XLA Ops:
  7.9 0.7 bitcast_compare_fusion
  10.4 1.0 fusion.29
  11.4 9.3 %psum.42 = f32[64]{0:T(128)S(1)} all-reduce(f32[64]{0:T(128)S(1)} %fusion.29), channel_id=1, replica_groups=mesh['sect'=64,'tp'=4] {'tp'}, use_global_device_ids=true, to_apply=%region_1.0 | all-reduce | flops 64 | bytes 512 | tf_op jit(solution)/shard_map/psum | solution.py:96
  20.7 1.0 fusion.31
  21.7 1.2 gather_fusion
  23.1 1.3 select_select_fusion
  24.4 14.3 %all-to-all-start = ((bf16[64,4,1024]{2,1,0:T(4,128)(2,1)}), bf16[64,4,1024]{2,1,0:T(4,128)(2,1)S(1)}, u32[]{:S(2)}, u32[]{:S(2)}) async-start(bf16[64,4,1024]{2,1,0:T(4,128)(2,1)} %select_select_fusion), calls=%async_computation | async-start | bytes 1048576 | tf_op jit(solution)/shard_map/all_to_all | solution.py:104
  38.9 19.4 %all-to-all-done = bf16[64,4,1024]{2,1,0:T(4,128)(2,1)S(1)} async-done(((bf16[64,4,1024]{2,1,0:T(4,128)(2,1)}), bf16[64,4,1024]{2,1,0:T(4,128)(2,1)S(1)}, u32[]{:S(2)}, u32[]{:S(2)}) %all-to-all-start) | async-done | bytes 524320 | tf_op jit(solution)/shard_map/all_to_all | solution.py:104
  58.9 6.0 %psum.43 = f32[256]{0:T(256)S(1)} all-reduce(f32[256]{0:T(256)S(1)} %reduce_sum.141), channel_id=1, replica_groups=mesh['sect'=64,'tp'=4] {'tp'}, use_global_device_ids=true, to_apply=%region_3.4 | all-reduce | flops 256 | bytes 2048 | tf_op jit(solution)/shard_map/psum | solution.py:108
  65.1 34.8 %all-gather.3.cloned.1.call-done = bf16[1024,4096]{0,1:T(8,128)(2,1)} async-done(((bf16[1024,64]{0,1:T(8,128)(2,1)}), bf16[1024,4096]{0,1:T(8,128)(2,1)}) %all-gather.3.cloned.1.call-update) | async-done | bytes 8388624 | tf_op jit(solution)/shard_map/all_gather | solution.py:118
  99.9 7.2 %convolution_convert_fusion = bf16[256,4096]{1,0:T(8,128)(2,1)} fusion(bf16[256,1024]{1,0:T(8,128)(2,1)S(1)} %multiply_convert_fusion.1, bf16[1024,4096]{0,1:T(8,128)(2,1)} %all-gather.3.cloned.1.call-done), kind=kOutput, calls=%fused_computation.14 | convolution fusion | flops 2148532224 | bytes 11010048 | tf_op jit(solution)/shard_map/dot_general | solution.py:116
  110.8 1.2 gather_fusion.5
  111.9 1.9 gather_fusion.6
  113.9 2.8 gather_fusion.2
  116.7 2.5 copy.131
  119.2 2.4 copy.110
  121.6 2.7 gather_fusion.1
  124.3 3.4 %copy.133 = f32[64,8,8,128]{3,2,1,0:T(8,128)} copy(f32[64,8,8,128]{3,1,2,0:T(8,128)} %bitcast.107) | data formatting | bytes 4194304
  127.6 3.1 copy.113
  130.8 1.6 slice.40
  132.5 3.5 %gather_fusion.4 = f32[512]{0:T(512)S(1)} fusion(f32[256]{0:T(256)S(1)} %psum.43, s32[1024]{0:T(1024)S(1)} %pad_clamp_fusion.1), kind=kCustom, calls=%fused_computation.4 | custom fusion | bytes 6144 | tf_op jit(solution)/shard_map/gather | solution.py:144
  136.2 1.1 convert_element_type.125
  137.4 2.7 gather_fusion.3
  140.1 2.1 copy.132
  142.1 1.4 multiply_reduce_fusion.1
  143.5 1.0 copy.105
  144.6 1.9 copy.106
  146.6 2.8 fusion.20
  150.1 0.8 fusion.18
  150.9 1.9 copy.112
  152.8 3.2 multiply_reduce_fusion
  156.0 2.0 convolution_convert_fusion.5
  158.1 8.6 %all-reduce.2 = (bf16[4,128]{1,0:T(4,128)(2,1)S(1)}, bf16[4,128]{1,0:T(4,128)(2,1)S(1)}) all-reduce(bf16[4,128]{1,0:T(4,128)(2,1)S(1)} %get-tuple-element.27, bf16[4,128]{1,0:T(4,128)(2,1)S(1)} %get-tuple-element.10), channel_id=1, replica_groups=mesh['sect'=64,'tp'=4] {'tp'}, use_global_device_ids=true, to_apply=%region_11.12 | all-reduce | flops 1024 | bytes 4096 | tf_op jit(solution)/shard_map/psum | solution.py:140
  167.3 34.6 %all-reduce.5.cloned.1.call-done = bf16[4,128,64]{1,2,0:T(8,128)(2,1)} async-done(((bf16[4,128,64]{1,2,0:T(8,128)(2,1)}), bf16[4,128,64]{1,2,0:T(8,128)(2,1)}) %all-reduce.5.cloned.1.call-update) | async-done | bytes 65552 | tf_op jit(solution)/shard_map/psum | solution.py:142
  201.9 1.0 fusion.38
  202.8 1.3 fusion.64
  205.0 0.8 fusion.40
  205.9 3.5 %pad_add_fusion = (f32[4,128,1024]{2,1,0:T(8,128)}, bf16[4,128,1024]{2,1,0:T(8,128)(2,1)}) fusion(f32[4,127,1024]{2,1,0:T(8,128)S(1)} %slice_multiply_fusion, f32[4,128,1024]{2,1,0:T(8,128)S(1)} %get-tuple-element.11, f32[4,128]{1,0:T(4,128)S(1)} %multiply_multiply_fusion.5, f32[4,127,1024]{2,1,0:T(8,128)S(1)} %copy-done.3, ...), kind=kOutput, calls=%fused_computation.48 | convolution fusion | flops 406552576 | bytes 10005504 | tf_op jit(solution)/shard_map/transpose(jvp(uif,ucf->uic))/dot_general | solution.py:50
  209.3 2.3 copy.130
  211.6 3.2 fusion.5
  215.4 1.1 fusion.16
  216.6 1.9 add_add_fusion.1
  218.5 2.9 copy.120
  221.4 7.5 %scatter_custom_fusion.2 = f32[256,1024]{1,0:T(8,128)} fusion(s32[512]{0:T(512)} %get-tuple-element.20, f32[64,8,8,128]{3,2,1,0:T(8,128)} %bitcast.114, f32[]{:T(128)} %constant.17.clone.1), kind=kCustom, calls=%fused_computation.37 | custom fusion | flops 524288 | bytes 3146240 | tf_op jit(solution)/shard_map/scatter-add | solution.py:89
  228.9 2.1 convert_element_type.143
  231.2 4.3 %fusion.9 = (f32[4,128,8]{1,2,0:T(8,128)S(1)}, bf16[4,8,128,128]{2,3,1,0:T(8,128)(2,1)S(1)}) fusion(bf16[4,128,8,128]{1,3,2,0:T(8,128)(2,1)} %copy.110, f32[4,128,8,128]{1,3,2,0:T(8,128)} %copy-done.1, f32[4,128,8]{1,2,0:T(8,128)S(1)} %get-tuple-element.37, bf16[4,8,128,128]{2,3,1,0:T(8,128)(2,1)} %copy-done.17, f32[4,8,128,128]{2,3,1,0:T(8,128)} %copy-done.9, ...), kind=kOutput, calls=%fused_computation.33 | convolution fusion | flops 141553664 | bytes 7667712 | tf_op jit(solution)/shard_map/transpose(jvp(uihd,ujhd->uhij))/dot_general | solution.py:31
  235.5 2.4 fusion.6
  237.9 3.0 copy.123
  241.0 2.3 scatter_custom_fusion.5
  243.3 2.3 fusion.43
  245.6 4.4 %scatter_custom_fusion.1 = f32[256,1024]{1,0:T(8,128)} fusion(s32[256]{0:T(256)S(1)} %reshape.374, f32[256,1024]{1,0:T(8,128)} %bitcast.124, f32[]{:T(128)} %constant.17.clone.1), kind=kCustom, calls=%fused_computation.68 | custom fusion | flops 262144 | bytes 1049088 | tf_op jit(solution)/shard_map/scatter-add | solution.py:89
  250.0 6.8 %scatter_custom_fusion = f32[256,1024]{1,0:T(8,128)} fusion(s32[512]{0:T(512)} %get-tuple-element.20, f32[512,1024]{1,0:T(8,128)} %bitcast.123, f32[]{:T(128)} %constant.17.clone.1), kind=kCustom, calls=%fused_computation.70 | custom fusion | flops 524288 | bytes 1049088 | tf_op jit(solution)/shard_map/scatter-add | solution.py:89
  256.8 4.2 %scatter_custom_fusion.4 = f32[256]{0:T(256)S(1)} fusion(s32[512]{0:T(512)S(1)} %add_bitcast_fusion, f32[512]{0:T(512)} %get-tuple-element.6, f32[]{:T(128)} %constant.17.clone.1), kind=kCustom, calls=%fused_computation.158 | custom fusion | flops 512 | bytes 1536 | tf_op jit(solution)/shard_map/scatter-add | solution.py:89
  261.1 5.7 %all-gather.5.cloned.1.call-done = bf16[256,4096]{1,0:T(8,128)(2,1)} async-done(((bf16[256,1024]{1,0:T(8,128)(2,1)}), bf16[256,4096]{1,0:T(8,128)(2,1)}) %all-gather.5.cloned.1.call-update) | async-done | bytes 2097168 | tf_op jit(solution)/shard_map/all_gather | solution.py:171
  266.8 7.4 %fusion.78 = f32[256,1024]{1,0:T(8,128)} fusion(bf16[256,4096]{1,0:T(8,128)(2,1)} %all-gather.5.cloned.1.call-done, bf16[1024,4096]{0,1:T(8,128)(2,1)} %all-gather.3.cloned.1.call-done), kind=kOutput, calls=%fused_computation.172 | convolution fusion | flops 2147483648 | bytes 11534336 | tf_op jit(solution)/shard_map/dot_general | solution.py:172
  274.2 7.4 %scatter_custom_fusion.3 = f32[256,1024]{1,0:T(8,128)} fusion(f32[256,1024]{1,0:T(8,128)} %fusion.78, s32[512]{0:T(512)} %get-tuple-element.20, f32[64,8,8,128]{3,2,1,0:T(8,128)S(1)} %bitcast.113), kind=kCustom, calls=%fused_computation.34 | custom fusion | flops 524288 | bytes 3145728 | tf_op jit(solution)/shard_map/scatter-add | solution.py:89
  281.6 1.5 multiply_reduce_fusion.2
  283.1 6.6 %psum.47 = f32[256]{0:T(256)S(1)} all-reduce(f32[256]{0:T(256)S(1)} %multiply_multiply_fusion.7), channel_id=1, replica_groups=mesh['sect'=64,'tp'=4] {'tp'}, use_global_device_ids=true, to_apply=%region_26.27 | all-reduce | flops 256 | bytes 2048 | tf_op jit(solution)/shard_map/psum | solution.py:180
  289.7 1.9 add_convert_fusion
  291.7 1.0 convert_element_type.151
  292.7 12.9 %all-to-all-start.1 = ((bf16[64,4,1024]{2,1,0:T(4,128)(2,1)}), bf16[64,4,1024]{2,1,0:T(4,128)(2,1)S(1)}, u32[]{:S(2)}, u32[]{:S(2)}) async-start(bf16[64,4,1024]{2,1,0:T(4,128)(2,1)} %convert_element_type.151), calls=%async_computation.2 | async-start | bytes 1048576 | tf_op jit(solution)/shard_map/all_to_all | solution.py:182
  306.3 16.9 %all-to-all-done.1 = bf16[64,4,1024]{2,1,0:T(4,128)(2,1)S(1)} async-done(((bf16[64,4,1024]{2,1,0:T(4,128)(2,1)}), bf16[64,4,1024]{2,1,0:T(4,128)(2,1)S(1)}, u32[]{:S(2)}, u32[]{:S(2)}) %all-to-all-start.1) | async-done | bytes 524320 | tf_op jit(solution)/shard_map/all_to_all | solution.py:182
  323.3 2.7 scatter_custom_fusion.6
  326.0 0.7 slice.42
  (148 shorter events, 11.4 us)
Async XLA Ops:
  7.2 92.7 %all-gather.3.cloned.1.call-start = ((), (), s32[]{:S(2)}) async-start(), calls=%async_computation.3 | async-start | bytes 8519680 | tf_op jit(solution)/shard_map/all_gather | solution.py:118
  22.9 15.9 %copy-start.39 = (bf16[1024]{0:T(1024)(128)(2,1)S(1)}, bf16[1024]{0:T(1024)(128)(2,1)}, u32[]{:S(2)}) copy-start(bf16[1024]{0:T(1024)(128)(2,1)} %param.12) | copy-start | bytes 6148
  24.4 33.8 %all-to-all-start = ((bf16[64,4,1024]{2,1,0:T(4,128)(2,1)}), bf16[64,4,1024]{2,1,0:T(4,128)(2,1)S(1)}, u32[]{:S(2)}, u32[]{:S(2)}) async-start(bf16[64,4,1024]{2,1,0:T(4,128)(2,1)} %select_select_fusion), calls=%async_computation | async-start | bytes 1048576 | tf_op jit(solution)/shard_map/all_to_all | solution.py:104
  38.8 97.4 %reduce-scatter.2.cloned.1.call-start = ((), (), s32[]{:S(2)}) async-start(), calls=%async_computation.4 | async-start | bytes 2621440 | tf_op jit(solution)/shard_map/reduce_scatter | solution.py:121
  64.9 35.0 %copy-start.31 = (f32[256]{0:T(256)}, f32[256]{0:T(256)S(1)}, u32[]{:S(2)}) copy-start(f32[256]{0:T(256)S(1)} %fusion.65) | copy-start | bytes 3076
  107.1 0.7 copy-start.26
  107.1 3.3 copy-start.41
  107.1 94.7 %all-reduce.5.cloned.1.call-start = ((), (), s32[]{:S(2)}) async-start(), calls=%async_computation.5 | async-start | bytes 131072 | tf_op jit(solution)/shard_map/psum | solution.py:142
  113.9 18.5 %copy-start.29 = (f32[256]{0:T(256)}, f32[256]{0:T(256)S(1)}, u32[]{:S(2)}) copy-start(f32[256]{0:T(256)S(1)} %gather_fusion.6) | copy-start | bytes 3076
  127.6 3.1 copy-start
  132.4 3.6 %copy-start.5 = (bf16[4,128,8,128]{1,3,2,0:T(8,128)(2,1)S(1)}, bf16[4,128,8,128]{1,3,2,0:T(8,128)(2,1)}, u32[]{:S(2)}) copy-start(bf16[4,128,8,128]{1,3,2,0:T(8,128)(2,1)} %copy.110) | copy-start | bytes 3145732
  142.1 2.4 copy-start.4
  146.5 2.9 copy-start.1
  146.5 2.9 copy-start.19
  146.5 3.5 %copy-start.6 = (bf16[4,128,8,128]{1,3,2,0:T(8,128)(2,1)S(1)}, bf16[4,128,8,128]{1,3,2,0:T(8,128)(2,1)}, u32[]{:S(2)}) copy-start(bf16[4,128,8,128]{1,3,2,0:T(8,128)(2,1)} %copy.110) | copy-start | bytes 3145732
  146.5 3.5 %copy-start.15 = (f32[4,128,8,128]{1,3,2,0:T(8,128)S(1)}, f32[4,128,8,128]{1,3,2,0:T(8,128)}, u32[]{:S(2)}) copy-start(f32[4,128,8,128]{1,3,2,0:T(8,128)} %copy.113) | copy-start | bytes 6291460
  149.4 1.5 copy-start.9
  158.0 108.7 %all-gather.5.cloned.1.call-start = ((), (), s32[]{:S(2)}) async-start(), calls=%async_computation.6 | async-start | bytes 2621440 | tf_op jit(solution)/shard_map/all_gather | solution.py:171
  166.7 37.5 %copy-start.27 = (bf16[4,128]{1,0:T(4,128)(2,1)}, bf16[4,128]{1,0:T(4,128)(2,1)S(1)}, u32[]{:S(2)}) copy-start(bf16[4,128]{1,0:T(4,128)(2,1)S(1)} %get-tuple-element.4) | copy-start | bytes 3076
  166.7 37.5 %copy-start.33 = (bf16[4,128]{1,0:T(4,128)(2,1)}, bf16[4,128]{1,0:T(4,128)(2,1)S(1)}, u32[]{:S(2)}) copy-start(bf16[4,128]{1,0:T(4,128)(2,1)S(1)} %get-tuple-element.5) | copy-start | bytes 3076
  204.1 1.7 copy-start.21
  204.2 0.8 copy-start.16
  204.2 1.6 copy-start.28
  204.2 1.6 copy-start.34
  204.2 1.6 copy-start.3
  204.2 1.6 copy-start.24
  209.3 2.3 copy-start.18
  211.6 3.3 copy-start.2
  211.6 3.3 copy-start.7
  211.6 3.8 %copy-start.10 = (f32[4,8,128,128]{2,3,1,0:T(8,128)S(1)}, f32[4,8,128,128]{2,3,1,0:T(8,128)}, u32[]{:S(2)}) copy-start(f32[4,8,128,128]{2,3,1,0:T(8,128)} %copy-done.9) | copy-start | bytes 6291460
  211.6 3.8 %copy-start.20 = (f32[4,128,8]{1,2,0:T(8,128)S(1)}, f32[4,128,8]{1,2,0:T(8,128)}, u32[]{:S(2)}) copy-start(f32[4,128,8]{1,2,0:T(8,128)} %copy-done.19) | copy-start | bytes 49156
  214.9 1.6 copy-start.17
  221.4 9.6 %copy-start.37 = (s32[4,64]{1,0:T(4,128)S(1)}, s32[4,64]{1,0:T(4,128)}, u32[]{:S(2)}) copy-start(s32[4,64]{1,0:T(4,128)} %get-tuple-element.17) | copy-start | bytes 3076
  221.4 9.7 %copy-start.35 = (s32[4,127]{1,0:T(4,128)S(1)}, s32[4,127]{1,0:T(4,128)}, u32[]{:S(2)}) copy-start(s32[4,127]{1,0:T(4,128)} %get-tuple-element.13) | copy-start | bytes 6100
  221.4 9.7 %copy-start.36 = (s32[4,1]{1,0:T(4,128)S(1)}, s32[4,1]{1,0:T(4,128)}, u32[]{:S(2)}) copy-start(s32[4,1]{1,0:T(4,128)} %get-tuple-element.15) | copy-start | bytes 52
  231.2 4.3 %copy-start.8 = (bf16[4,128,8,128]{1,3,2,0:T(8,128)(2,1)S(1)}, bf16[4,128,8,128]{1,3,2,0:T(8,128)(2,1)}, u32[]{:S(2)}) copy-start(bf16[4,128,8,128]{1,3,2,0:T(8,128)(2,1)} %copy.110) | copy-start | bytes 3145732
  231.2 4.3 %copy-start.11 = (f32[4,8,128,128]{2,3,1,0:T(8,128)S(1)}, f32[4,8,128,128]{2,3,1,0:T(8,128)}, u32[]{:S(2)}) copy-start(f32[4,8,128,128]{2,3,1,0:T(8,128)} %copy-done.9) | copy-start | bytes 6291460
  231.2 4.3 %copy-start.14 = (bf16[4,128,1024]{1,2,0:T(8,128)(2,1)S(1)}, bf16[4,128,1024]{1,2,0:T(8,128)(2,1)}, u32[]{:S(2)}) copy-start(bf16[4,128,1024]{1,2,0:T(8,128)(2,1)} %copy.130) | copy-start | bytes 3145732
  237.9 3.0 copy-start.38
  237.9 3.1 copy-start.30
  237.9 5.4 %copy-start.22 = (f32[4,128]{1,0:T(4,128)S(1)}, f32[4,128]{1,0:T(4,128)}, u32[]{:S(2)}) copy-start(f32[4,128]{1,0:T(4,128)} %copy-done.21) | copy-start | bytes 6148
  237.9 5.4 %copy-start.25 = (f32[4,128]{1,0:T(4,128)S(1)}, f32[4,128]{1,0:T(4,128)}, u32[]{:S(2)}) copy-start(f32[4,128]{1,0:T(4,128)} %get-tuple-element.23) | copy-start | bytes 6148
  261.0 13.1 %copy-start.12 = (f32[4,128,8,128]{3,2,1,0:T(8,128)S(1)}, f32[4,128,8,128]{3,2,1,0:T(8,128)}, u32[]{:S(2)}) copy-start(f32[4,128,8,128]{3,2,1,0:T(8,128)} %copy.123) | copy-start | bytes 6291460
  274.2 15.6 %copy-start.32 = (f32[256]{0:T(256)S(1)}, f32[256]{0:T(256)}, u32[]{:S(2)}) copy-start(f32[256]{0:T(256)} %copy-done.31) | copy-start | bytes 3076
  281.6 8.2 %copy-start.13 = (f32[256,1024]{1,0:T(8,128)S(1)}, f32[256,1024]{1,0:T(8,128)}, u32[]{:S(2)}) copy-start(f32[256,1024]{1,0:T(8,128)} %scatter_custom_fusion.1) | copy-start | bytes 3145732
  291.7 13.9 %copy-start.23 = (s32[1,64,4]{1,2,0:T(4,128)S(1)}, s32[1,64,4]{1,2,0:T(4,128)}, u32[]{:S(2)}) copy-start(s32[1,64,4]{1,2,0:T(4,128)} %param.9) | copy-start | bytes 3076
  291.7 14.1 %copy-start.40 = (f32[4]{0:T(128)S(1)}, f32[4]{0:T(128)}, u32[]{:S(2)}) copy-start(f32[4]{0:T(128)} %get-tuple-element.12) | copy-start | bytes 52
  291.7 14.1 %copy-start.42 = (s32[4]{0:T(128)S(1)}, s32[4]{0:T(128)}, u32[]{:S(2)}) copy-start(s32[4]{0:T(128)} %param.11) | copy-start | bytes 52
  292.7 30.5 %all-to-all-start.1 = ((bf16[64,4,1024]{2,1,0:T(4,128)(2,1)}), bf16[64,4,1024]{2,1,0:T(4,128)(2,1)S(1)}, u32[]{:S(2)}, u32[]{:S(2)}) async-start(bf16[64,4,1024]{2,1,0:T(4,128)(2,1)} %convert_element_type.151), calls=%async_computation.2 | async-start | bytes 1048576 | tf_op jit(solution)/shard_map/all_to_all | solution.py:182
Sparse Core Ops, SparseCore 0:
  10.7 89.1 all-gather.2
  107.3 28.5 reduce-scatter.1
  158.1 43.6 all-reduce.4
  231.1 35.5 all-gather.4
where the time goes:
time: 339 us; the launch traced here: 333 us
  waiting for transfers between devices  112 us (33%)
  other arithmetic  61.6 us (18%)
  local copies, waits for them, and re-layouts  50 us (15%)
  matrix products  37 us (11%)
  blocking collectives  30.5 us (9%)
  starting transfers between devices  27.5 us (8%)
  between operations  14.6 us (4%)
    all_gather x1, waiting for transfers between devices, local(): lax.all_gather(query_weight, 'sect', axis=1, tiled=True)  34.8 us
    psum x1, waiting for transfers between devices, local(): lax.psum(partial_stats[2].astype(jnp.bfloat16), 'tp').astype(jnp.float32)  34.6 us
    scatter-add x6, other arithmetic, segment_rows(): jax.ops.segment_sum(values.reshape((-1,) + values.shape[2:]), places.resh...  32.6 us
    all_to_all x1, waiting for transfers between devices, local(): lax.all_to_all(outgoing, 'sect', split_axis=0, concat_axis=0, tiled=True)  19.4 us
    all_to_all x1, waiting for transfers between devices, local(): lax.all_to_all(grad_slots.reshape(arrived.shape).astype(jnp.bfloat16), 's...  16.9 us
    all_to_all x1, starting transfers between devices, local(): lax.all_to_all(outgoing, 'sect', split_axis=0, concat_axis=0, tiled=True)  14.3 us
    all_to_all x1, starting transfers between devices, local(): lax.all_to_all(grad_slots.reshape(arrived.shape).astype(jnp.bfloat16), 's...  12.9 us
    unnamed x90, local copies, waits for them, and re-layouts  9.68 us
  transfers between devices with their start and end apart: 6, of which 5 were waited for; matrix products, arithmetic and copies ran while one was open for 20% of the time, Pallas kernels for 0%

commit v1 on v0

--- a/solution.py
+++ b/solution.py
@@ -139,7 +139,9 @@
     own_squares, positive_dot_products, negative_dot_products = (
         lax.psum(partial_stats[0].astype(jnp.bfloat16), "tp").astype(jnp.float32),
         lax.psum(partial_stats[1].astype(jnp.bfloat16), "tp").astype(jnp.float32),
-        lax.psum(partial_stats[2].astype(jnp.bfloat16), "tp").astype(jnp.float32),
+        jnp.sum(lax.all_gather(partial_stats[2].astype(jnp.bfloat16), "tp"), axis=0).astype(
+            jnp.float32
+        ),
     )
     next_item_square_sums = slot_squares[follow_places]
     candidate_square_sums = slot_squares[cand_places]

time: 339 us -> 317 us (0.935)
  waiting for transfers between devices: 112 us -> 75.1 us
  blocking collectives: 30.5 us -> 41.1 us
    psum x1 -> x0, waiting for transfers between devices: 34.6 us -> none  [local(): lax.psum(partial_stats[2].astype(jnp.bfloat16), 'tp').astype(jnp.float32)]
    all_gather x0 -> x1, blocking collectives: none -> 10.4 us  [local(): lax.all_gather(partial_stats[2].astype(jnp.bfloat16), 'tp')]
    unnamed x90 -> x86, local copies, waits for them, and re-layouts: 9.68 us -> 11 us
  transfers between devices with their start and end apart: 6 -> 5, of which waited for: 5 -> 4; matrix products, arithmetic and copies ran while one was open for 20% -> 22% of each run, Pallas kernels for 0% -> 0%
where the time goes in v1:
time: 317 us; the launch traced here: 311 us
  waiting for transfers between devices  75.1 us (24%)
  other arithmetic  64.2 us (20%)
  local copies, waits for them, and re-layouts  52.5 us (17%)
  blocking collectives  41.1 us (13%)
  matrix products  36.3 us (11%)
  starting transfers between devices  27.5 us (9%)
  between operations  14.5 us (5%)
    all_gather x1, waiting for transfers between devices, local(): lax.all_gather(query_weight, 'sect', axis=1, tiled=True)  34.5 us
    scatter-add x6, other arithmetic, segment_rows(): jax.ops.segment_sum(values.reshape((-1,) + values.shape[2:]), places.resh...  32.6 us
    all_to_all x1, waiting for transfers between devices, local(): lax.all_to_all(outgoing, 'sect', split_axis=0, concat_axis=0, tiled=True)  19.4 us
    all_to_all x1, waiting for transfers between devices, local(): lax.all_to_all(grad_slots.reshape(arrived.shape).astype(jnp.bfloat16), 's...  16.9 us
    all_to_all x1, starting transfers between devices, local(): lax.all_to_all(outgoing, 'sect', split_axis=0, concat_axis=0, tiled=True)  14.3 us
    all_to_all x1, starting transfers between devices, local(): lax.all_to_all(grad_slots.reshape(arrived.shape).astype(jnp.bfloat16), 's...  12.9 us
    unnamed x86, local copies, waits for them, and re-layouts  11 us
    all_gather x1, blocking collectives, local(): lax.all_gather(partial_stats[2].astype(jnp.bfloat16), 'tp')  10.4 us
  transfers between devices with their start and end apart: 5, of which 4 were waited for; matrix products, arithmetic and copies ran while one was open for 22% of the time, Pallas kernels for 0%

profile of v1, /device:TPU:1, one launch (start us, length us, event | category | flops | bytes accessed | tf_op | source)
XLA Modules:
  0.0 311.2 jit_solution(15119186434482865559)
XLA Ops:
  10.4 1.0 fusion.29
  11.4 9.3 %psum.35 = f32[64]{0:T(128)S(1)} all-reduce(f32[64]{0:T(128)S(1)} %fusion.29), channel_id=1, replica_groups=mesh['sect'=64,'tp'=4] {'tp'}, use_global_device_ids=true, to_apply=%region_1.0 | all-reduce | flops 64 | bytes 512 | tf_op jit(solution)/shard_map/psum | solution.py:96
  20.7 1.0 fusion.31
  21.7 1.2 gather_fusion
  23.1 1.3 select_select_fusion
  24.4 14.3 %all-to-all-start = ((bf16[64,4,1024]{2,1,0:T(4,128)(2,1)}), bf16[64,4,1024]{2,1,0:T(4,128)(2,1)S(1)}, u32[]{:S(2)}, u32[]{:S(2)}) async-start(bf16[64,4,1024]{2,1,0:T(4,128)(2,1)} %select_select_fusion), calls=%async_computation | async-start | bytes 1048576 | tf_op jit(solution)/shard_map/all_to_all | solution.py:104
  38.9 19.4 %all-to-all-done = bf16[64,4,1024]{2,1,0:T(4,128)(2,1)S(1)} async-done(((bf16[64,4,1024]{2,1,0:T(4,128)(2,1)}), bf16[64,4,1024]{2,1,0:T(4,128)(2,1)S(1)}, u32[]{:S(2)}, u32[]{:S(2)}) %all-to-all-start) | async-done | bytes 524320 | tf_op jit(solution)/shard_map/all_to_all | solution.py:104
  58.9 6.0 %psum.36 = f32[256]{0:T(256)S(1)} all-reduce(f32[256]{0:T(256)S(1)} %reduce_sum.177), channel_id=1, replica_groups=mesh['sect'=64,'tp'=4] {'tp'}, use_global_device_ids=true, to_apply=%region_3.4 | all-reduce | flops 256 | bytes 2048 | tf_op jit(solution)/shard_map/psum | solution.py:108
  65.1 34.5 %all-gather.4.cloned.1.call-done = bf16[1024,4096]{0,1:T(8,128)(2,1)} async-done(((bf16[1024,64]{0,1:T(8,128)(2,1)}), bf16[1024,4096]{0,1:T(8,128)(2,1)}) %all-gather.4.cloned.1.call-update) | async-done | bytes 8388624 | tf_op jit(solution)/shard_map/all_gather | solution.py:118
  99.6 7.2 %convolution_convert_fusion = bf16[256,4096]{1,0:T(8,128)(2,1)} fusion(bf16[256,1024]{1,0:T(8,128)(2,1)S(1)} %multiply_convert_fusion.1, bf16[1024,4096]{0,1:T(8,128)(2,1)} %all-gather.4.cloned.1.call-done), kind=kOutput, calls=%fused_computation.14 | convolution fusion | flops 2148532224 | bytes 11010048 | tf_op jit(solution)/shard_map/dot_general | solution.py:116
  111.5 1.2 gather_fusion.5
  112.6 1.9 gather_fusion.6
  114.6 2.8 gather_fusion.2
  117.4 2.5 copy.131
  119.9 2.4 copy.110
  122.3 2.7 gather_fusion.1
  125.0 3.4 %copy.133 = f32[64,8,8,128]{3,2,1,0:T(8,128)} copy(f32[64,8,8,128]{3,1,2,0:T(8,128)} %bitcast.108) | data formatting | bytes 4194304
  128.4 3.1 copy.113
  131.5 1.6 slice.40
  133.2 4.7 %gather_fusion.4 = f32[512]{0:T(512)} fusion(f32[256]{0:T(256)S(1)} %psum.36, s32[1024]{0:T(1024)S(1)} %pad_clamp_fusion.1), kind=kCustom, calls=%fused_computation.4 | custom fusion | bytes 6144 | tf_op jit(solution)/shard_map/gather | solution.py:146
  138.1 1.1 convert_element_type.127
  139.3 2.7 gather_fusion.3
  141.9 2.1 copy.132
  144.0 1.4 multiply_reduce_fusion.1
  145.4 1.0 copy.105
  146.4 1.9 copy.106
  148.4 2.8 fusion.20
  151.4 0.8 fusion.18
  152.6 1.9 copy.112
  154.5 3.2 %multiply_reduce_fusion = (bf16[4,128]{1,0:T(4,128)(2,1)S(1)}, f32[4,128,1024]{2,1,0:T(8,128)S(1)}) fusion(f32[4,127,1024]{2,1,0:T(8,128)} %slice.40, f32[4,128,1024]{2,1,0:T(8,128)} %bitcast.109, f32[4,128,1024]{2,1,0:T(8,128)} %copy.112), kind=kLoop, calls=%fused_computation.49 | loop fusion | flops 1572352 | bytes 8373248 | tf_op jit(solution)/shard_map/jvp()/reduce_sum | solution.py:49
  157.7 1.3 convolution_convert_fusion.5
  159.1 10.4 %all-gather = bf16[16,128,64]{1,2,0:T(8,128)(2,1)} all-gather(bf16[4,128,64]{1,2,0:T(8,128)(2,1)S(1)} %convolution_convert_fusion.5), channel_id=2, replica_groups=mesh['sect'=64,'tp'=4] {'tp'}, dimensions={0}, use_global_device_ids=true | all-gather | bytes 327680 | tf_op jit(solution)/shard_map/all_gather | solution.py:142
  169.5 8.8 %all-reduce.2 = (bf16[4,128]{1,0:T(4,128)(2,1)S(1)}, bf16[4,128]{1,0:T(4,128)(2,1)}) all-reduce(bf16[4,128]{1,0:T(4,128)(2,1)S(1)} %get-tuple-element.27, bf16[4,128]{1,0:T(4,128)(2,1)S(1)} %get-tuple-element.10), channel_id=1, replica_groups=mesh['sect'=64,'tp'=4] {'tp'}, use_global_device_ids=true, to_apply=%region_11.12 | all-reduce | flops 1024 | bytes 4096 | tf_op jit(solution)/shard_map/psum | solution.py:140
  178.9 1.0 reduce_sum.183
  180.0 2.1 fusion.64
  182.1 0.8 fusion.40
  182.9 0.8 multiply_multiply_fusion.6
  184.9 0.9 copy-done.3
  185.9 3.5 %pad_add_fusion = (f32[4,128,1024]{2,1,0:T(8,128)}, bf16[4,128,1024]{2,1,0:T(8,128)(2,1)}) fusion(f32[4,127,1024]{2,1,0:T(8,128)S(1)} %slice_multiply_fusion, f32[4,128,1024]{2,1,0:T(8,128)S(1)} %get-tuple-element.11, f32[4,128]{1,0:T(4,128)S(1)} %multiply_multiply_fusion.5, f32[4,127,1024]{2,1,0:T(8,128)S(1)} %copy-done.3, ...), kind=kOutput, calls=%fused_computation.48 | convolution fusion | flops 406552576 | bytes 10005504 | tf_op jit(solution)/shard_map/transpose(jvp(uif,ucf->uic))/dot_general | solution.py:50
  189.3 2.3 copy.130
  191.6 3.2 %fusion.5 = (f32[4,8,128]{2,1,0:T(8,128)S(1)}, bf16[4,8,128,128]{2,3,1,0:T(8,128)(2,1)S(1)}) fusion(f32[4,8,128,128]{2,3,1,0:T(8,128)} %copy-done.9, f32[4,8,128]{2,1,0:T(8,128)S(1)} %copy-done.17, f32[4,128,128]{1,2,0:T(8,128)S(1)} %and_convert_fusion, bf16[4,8,128,128]{3,2,1,0:T(8,128)(2,1)} %bitcast.121, bf16[4,128,8,128]{1,3,2,0:T(8,128)(2,1)} %copy.110), kind=kOutput, calls=%fused_computation.29 | convolution fusion | flops 137359360 | bytes 5537792 | tf_op jit(solution)/shard_map/transpose(jvp(uhij,ujhd->uihd))/dot_general | solution.py:36
  195.4 1.1 fusion.16
  196.6 1.9 add_add_fusion.1
  198.5 2.9 copy.120
  201.4 7.5 %scatter_custom_fusion.2 = f32[256,1024]{1,0:T(8,128)} fusion(s32[512]{0:T(512)} %get-tuple-element.20, f32[64,8,8,128]{3,2,1,0:T(8,128)} %bitcast.115, f32[]{:T(128)} %constant.17.clone.1), kind=kCustom, calls=%fused_computation.37 | custom fusion | flops 524288 | bytes 3146240 | tf_op jit(solution)/shard_map/scatter-add | solution.py:89
  208.9 2.1 convert_element_type.145
  211.2 4.3 %fusion.9 = (f32[4,128,8]{1,2,0:T(8,128)S(1)}, bf16[4,8,128,128]{2,3,1,0:T(8,128)(2,1)S(1)}) fusion(bf16[4,128,8,128]{1,3,2,0:T(8,128)(2,1)} %copy.110, f32[4,128,8,128]{1,3,2,0:T(8,128)} %copy-done.1, f32[4,128,8]{1,2,0:T(8,128)S(1)} %get-tuple-element.37, bf16[4,8,128,128]{2,3,1,0:T(8,128)(2,1)} %copy-done.16, f32[4,8,128,128]{2,3,1,0:T(8,128)} %copy-done.9, ...), kind=kOutput, calls=%fused_computation.33 | convolution fusion | flops 141553664 | bytes 7667712 | tf_op jit(solution)/shard_map/transpose(jvp(uihd,ujhd->uhij))/dot_general | solution.py:31
  215.5 2.4 fusion.6
  217.9 3.0 copy.123
  221.0 2.3 scatter_custom_fusion.5
  223.3 2.3 fusion.43
  225.6 4.3 %scatter_custom_fusion.1 = f32[256,1024]{1,0:T(8,128)} fusion(s32[256]{0:T(256)S(1)} %reshape.374, f32[256,1024]{1,0:T(8,128)} %bitcast.125, f32[]{:T(128)} %constant.17.clone.1), kind=kCustom, calls=%fused_computation.68 | custom fusion | flops 262144 | bytes 1049088 | tf_op jit(solution)/shard_map/scatter-add | solution.py:89
  229.9 6.8 %scatter_custom_fusion = f32[256,1024]{1,0:T(8,128)} fusion(s32[512]{0:T(512)} %get-tuple-element.20, f32[512,1024]{1,0:T(8,128)} %bitcast.124, f32[]{:T(128)} %constant.17.clone.1), kind=kCustom, calls=%fused_computation.70 | custom fusion | flops 524288 | bytes 1049088 | tf_op jit(solution)/shard_map/scatter-add | solution.py:89
  236.7 4.2 %scatter_custom_fusion.4 = f32[256]{0:T(256)S(1)} fusion(s32[512]{0:T(512)S(1)} %add_bitcast_fusion, f32[512]{0:T(512)} %get-tuple-element.6, f32[]{:T(128)} %constant.17.clone.1), kind=kCustom, calls=%fused_computation.158 | custom fusion | flops 512 | bytes 1536 | tf_op jit(solution)/shard_map/scatter-add | solution.py:89
  241.0 3.5 %all-gather.6.cloned.1.call-done = bf16[256,4096]{1,0:T(8,128)(2,1)} async-done(((bf16[256,1024]{1,0:T(8,128)(2,1)}), bf16[256,4096]{1,0:T(8,128)(2,1)}) %all-gather.6.cloned.1.call-update) | async-done | bytes 2097168 | tf_op jit(solution)/shard_map/all_gather | solution.py:173
  244.5 7.4 %fusion.78 = f32[256,1024]{1,0:T(8,128)} fusion(bf16[256,4096]{1,0:T(8,128)(2,1)} %all-gather.6.cloned.1.call-done, bf16[1024,4096]{0,1:T(8,128)(2,1)} %all-gather.4.cloned.1.call-done), kind=kOutput, calls=%fused_computation.172 | convolution fusion | flops 2147483648 | bytes 11534336 | tf_op jit(solution)/shard_map/dot_general | solution.py:174
  251.9 7.4 %scatter_custom_fusion.3 = f32[256,1024]{1,0:T(8,128)} fusion(f32[256,1024]{1,0:T(8,128)} %fusion.78, s32[512]{0:T(512)} %get-tuple-element.20, f32[64,8,8,128]{3,2,1,0:T(8,128)S(1)} %bitcast.114), kind=kCustom, calls=%fused_computation.34 | custom fusion | flops 524288 | bytes 3145728 | tf_op jit(solution)/shard_map/scatter-add | solution.py:89
  259.3 1.5 multiply_reduce_fusion.2
  260.9 6.6 %psum.39 = f32[256]{0:T(256)S(1)} all-reduce(f32[256]{0:T(256)S(1)} %multiply_multiply_fusion.7), channel_id=1, replica_groups=mesh['sect'=64,'tp'=4] {'tp'}, use_global_device_ids=true, to_apply=%region_26.27 | all-reduce | flops 256 | bytes 2048 | tf_op jit(solution)/shard_map/psum | solution.py:182
  267.5 1.9 add_convert_fusion
  269.4 1.0 convert_element_type.153
  270.4 12.9 %all-to-all-start.1 = ((bf16[64,4,1024]{2,1,0:T(4,128)(2,1)}), bf16[64,4,1024]{2,1,0:T(4,128)(2,1)S(1)}, u32[]{:S(2)}, u32[]{:S(2)}) async-start(bf16[64,4,1024]{2,1,0:T(4,128)(2,1)} %convert_element_type.153), calls=%async_computation.2 | async-start | bytes 1048576 | tf_op jit(solution)/shard_map/all_to_all | solution.py:184
  284.1 16.9 %all-to-all-done.1 = bf16[64,4,1024]{2,1,0:T(4,128)(2,1)S(1)} async-done(((bf16[64,4,1024]{2,1,0:T(4,128)(2,1)}), bf16[64,4,1024]{2,1,0:T(4,128)(2,1)S(1)}, u32[]{:S(2)}, u32[]{:S(2)}) %all-to-all-start.1) | async-done | bytes 524320 | tf_op jit(solution)/shard_map/all_to_all | solution.py:184
  301.1 2.7 scatter_custom_fusion.6
  (143 shorter events, 14.2 us)
Async XLA Ops:
  7.2 92.4 %all-gather.4.cloned.1.call-start = ((), (), s32[]{:S(2)}) async-start(), calls=%async_computation.3 | async-start | bytes 8519680 | tf_op jit(solution)/shard_map/all_gather | solution.py:118
  22.9 15.9 %copy-start.37 = (bf16[1024]{0:T(1024)(128)(2,1)S(1)}, bf16[1024]{0:T(1024)(128)(2,1)}, u32[]{:S(2)}) copy-start(bf16[1024]{0:T(1024)(128)(2,1)} %param.12) | copy-start | bytes 6148
  24.4 33.8 %all-to-all-start = ((bf16[64,4,1024]{2,1,0:T(4,128)(2,1)}), bf16[64,4,1024]{2,1,0:T(4,128)(2,1)S(1)}, u32[]{:S(2)}, u32[]{:S(2)}) async-start(bf16[64,4,1024]{2,1,0:T(4,128)(2,1)} %select_select_fusion), calls=%async_computation | async-start | bytes 1048576 | tf_op jit(solution)/shard_map/all_to_all | solution.py:104
  38.8 99.3 %reduce-scatter.2.cloned.1.call-start = ((), (), s32[]{:S(2)}) async-start(), calls=%async_computation.4 | async-start | bytes 2621440 | tf_op jit(solution)/shard_map/reduce_scatter | solution.py:121
  64.9 34.7 %copy-start.30 = (f32[256]{0:T(256)}, f32[256]{0:T(256)S(1)}, u32[]{:S(2)}) copy-start(f32[256]{0:T(256)S(1)} %fusion.65) | copy-start | bytes 3076
  106.8 0.7 copy-start.25
  106.8 3.3 %copy-start.39 = (s32[4]{0:T(128)S(1)}, s32[4]{0:T(128)}, u32[]{:S(2)}) copy-start(s32[4]{0:T(128)} %param.11) | copy-start | bytes 52
  106.8 137.7 %all-gather.6.cloned.1.call-start = ((), (), s32[]{:S(2)}) async-start(), calls=%async_computation.5 | async-start | bytes 2621440 | tf_op jit(solution)/shard_map/all_gather | solution.py:173
  114.6 18.5 %copy-start.28 = (f32[256]{0:T(256)}, f32[256]{0:T(256)S(1)}, u32[]{:S(2)}) copy-start(f32[256]{0:T(256)S(1)} %gather_fusion.6) | copy-start | bytes 3076
  128.4 3.1 copy-start
  133.1 4.8 %copy-start.5 = (bf16[4,128,8,128]{1,3,2,0:T(8,128)(2,1)S(1)}, bf16[4,128,8,128]{1,3,2,0:T(8,128)(2,1)}, u32[]{:S(2)}) copy-start(bf16[4,128,8,128]{1,3,2,0:T(8,128)(2,1)} %copy.110) | copy-start | bytes 3145732
  144.0 2.4 copy-start.4
  148.4 2.9 copy-start.1
  148.4 2.9 copy-start.18
  148.4 2.9 copy-start.6
  148.4 3.0 copy-start.15
  151.3 1.4 copy-start.9
  178.3 0.6 copy-start.26
  182.1 2.9 copy-start.20
  184.3 0.7 copy-start.27
  184.3 0.7 copy-start.32
  184.3 1.6 copy-start.3
  184.3 1.6 copy-start.23
  189.3 2.3 copy-start.17
  191.6 3.3 %copy-start.2 = (f32[4,128,8,128]{1,3,2,0:T(8,128)S(1)}, f32[4,128,8,128]{1,3,2,0:T(8,128)}, u32[]{:S(2)}) copy-start(f32[4,128,8,128]{1,3,2,0:T(8,128)} %copy-done.1) | copy-start | bytes 6291460
  191.6 3.3 %copy-start.7 = (bf16[4,128,8,128]{1,3,2,0:T(8,128)(2,1)S(1)}, bf16[4,128,8,128]{1,3,2,0:T(8,128)(2,1)}, u32[]{:S(2)}) copy-start(bf16[4,128,8,128]{1,3,2,0:T(8,128)(2,1)} %copy.110) | copy-start | bytes 3145732
  191.6 3.8 %copy-start.10 = (f32[4,8,128,128]{2,3,1,0:T(8,128)S(1)}, f32[4,8,128,128]{2,3,1,0:T(8,128)}, u32[]{:S(2)}) copy-start(f32[4,8,128,128]{2,3,1,0:T(8,128)} %copy-done.9) | copy-start | bytes 6291460
  191.6 3.8 %copy-start.19 = (f32[4,128,8]{1,2,0:T(8,128)S(1)}, f32[4,128,8]{1,2,0:T(8,128)}, u32[]{:S(2)}) copy-start(f32[4,128,8]{1,2,0:T(8,128)} %copy-done.18) | copy-start | bytes 49156
  194.9 1.6 copy-start.16
  201.4 9.6 %copy-start.35 = (s32[4,64]{1,0:T(4,128)S(1)}, s32[4,64]{1,0:T(4,128)}, u32[]{:S(2)}) copy-start(s32[4,64]{1,0:T(4,128)} %get-tuple-element.17) | copy-start | bytes 3076
  201.4 9.7 %copy-start.33 = (s32[4,127]{1,0:T(4,128)S(1)}, s32[4,127]{1,0:T(4,128)}, u32[]{:S(2)}) copy-start(s32[4,127]{1,0:T(4,128)} %get-tuple-element.13) | copy-start | bytes 6100
  201.4 9.7 %copy-start.34 = (s32[4,1]{1,0:T(4,128)S(1)}, s32[4,1]{1,0:T(4,128)}, u32[]{:S(2)}) copy-start(s32[4,1]{1,0:T(4,128)} %get-tuple-element.15) | copy-start | bytes 52
  211.2 4.3 %copy-start.8 = (bf16[4,128,8,128]{1,3,2,0:T(8,128)(2,1)S(1)}, bf16[4,128,8,128]{1,3,2,0:T(8,128)(2,1)}, u32[]{:S(2)}) copy-start(bf16[4,128,8,128]{1,3,2,0:T(8,128)(2,1)} %copy.110) | copy-start | bytes 3145732
  211.2 4.3 %copy-start.11 = (f32[4,8,128,128]{2,3,1,0:T(8,128)S(1)}, f32[4,8,128,128]{2,3,1,0:T(8,128)}, u32[]{:S(2)}) copy-start(f32[4,8,128,128]{2,3,1,0:T(8,128)} %copy-done.9) | copy-start | bytes 6291460
  211.2 4.3 %copy-start.14 = (bf16[4,128,1024]{1,2,0:T(8,128)(2,1)S(1)}, bf16[4,128,1024]{1,2,0:T(8,128)(2,1)}, u32[]{:S(2)}) copy-start(bf16[4,128,1024]{1,2,0:T(8,128)(2,1)} %copy.130) | copy-start | bytes 3145732
  217.9 3.0 copy-start.36
  217.9 3.1 copy-start.29
  217.9 5.4 %copy-start.21 = (f32[4,128]{1,0:T(4,128)S(1)}, f32[4,128]{1,0:T(4,128)}, u32[]{:S(2)}) copy-start(f32[4,128]{1,0:T(4,128)} %copy-done.20) | copy-start | bytes 6148
  217.9 5.4 %copy-start.24 = (f32[4,128]{1,0:T(4,128)S(1)}, f32[4,128]{1,0:T(4,128)}, u32[]{:S(2)}) copy-start(f32[4,128]{1,0:T(4,128)} %get-tuple-element.23) | copy-start | bytes 6148
  241.0 10.9 %copy-start.12 = (f32[4,128,8,128]{3,2,1,0:T(8,128)S(1)}, f32[4,128,8,128]{3,2,1,0:T(8,128)}, u32[]{:S(2)}) copy-start(f32[4,128,8,128]{3,2,1,0:T(8,128)} %copy.123) | copy-start | bytes 6291460
  251.9 15.5 %copy-start.31 = (f32[256]{0:T(256)S(1)}, f32[256]{0:T(256)}, u32[]{:S(2)}) copy-start(f32[256]{0:T(256)} %copy-done.30) | copy-start | bytes 3076
  259.3 8.1 %copy-start.13 = (f32[256,1024]{1,0:T(8,128)S(1)}, f32[256,1024]{1,0:T(8,128)}, u32[]{:S(2)}) copy-start(f32[256,1024]{1,0:T(8,128)} %scatter_custom_fusion.1) | copy-start | bytes 3145732
  269.4 13.9 %copy-start.22 = (s32[1,64,4]{1,2,0:T(4,128)S(1)}, s32[1,64,4]{1,2,0:T(4,128)}, u32[]{:S(2)}) copy-start(s32[1,64,4]{1,2,0:T(4,128)} %param.9) | copy-start | bytes 3076
  269.4 14.1 %copy-start.38 = (f32[4]{0:T(128)S(1)}, f32[4]{0:T(128)}, u32[]{:S(2)}) copy-start(f32[4]{0:T(128)} %get-tuple-element.12) | copy-start | bytes 52
  269.4 14.1 %copy-start.40 = (s32[4]{0:T(128)S(1)}, s32[4]{0:T(128)}, u32[]{:S(2)}) copy-start(s32[4]{0:T(128)} %param.11) | copy-start | bytes 52
  270.4 30.6 %all-to-all-start.1 = ((bf16[64,4,1024]{2,1,0:T(4,128)(2,1)}), bf16[64,4,1024]{2,1,0:T(4,128)(2,1)S(1)}, u32[]{:S(2)}, u32[]{:S(2)}) async-start(bf16[64,4,1024]{2,1,0:T(4,128)(2,1)} %convert_element_type.153), calls=%async_computation.2 | async-start | bytes 1048576 | tf_op jit(solution)/shard_map/all_to_all | solution.py:184
Sparse Core Ops, SparseCore 0:
  10.7 88.8 all-gather.3
  106.9 28.5 reduce-scatter.1
  211.1 33.3 all-gather.5
